TPU v7x, 128 devices: a whole 4x4x4 slice. The times are simulated.
128 devices in a mesh: group: 4 (over x), bulk: 32 (over z, y, core).
Axes of the slice: x: 4, y: 4, z: 4, core: 2. Of those that a mesh axis runs over, the one named last changes fastest.
Arguments:
- rhs: float32 [512, 64, 128], P(('group', 'bulk')), may hold values from -90 to 90, as said below
- diag_tiles: float32 [512, 128, 128], P(('group', 'bulk')), may hold values from -0.06 to 0.06
- offdiag_blocks: float32 [512, 11, 128, 128], P(('group', 'bulk')), may hold values from -0.026 to 0.026
- coupling: float32 [256, 4, 128, 128], P(('group', 'bulk')), may hold values from -0.05 to 0.05, as said below
- col_index: int32 [512, 11], replicated, may hold values from 0 to 511, as said below
- load: int32 [512], replicated, may hold values from 3 to 11
- new_slot: int32 [512], replicated, may hold values from 0 to 511, as said below
Outputs:
- solution_out: float32 [512, 64, 128], P(('group', 'bulk'))
- residual_out: float32 [512, 64, 128], P(('group', 'bulk'))
Inputs may be any that keep to these rules, and one draw needn't show every extreme that they name: `rhs`: made of random entries times scales of the rows and of the columns. `coupling`: entry [d * 2 + k, h] is the transpose of entry [(h * 32 + d % 32) * 2 + k, d // 32]. `col_index`: for each part g and each tile position t, the column t of the 128 block rows of part g is a permutation of that part's slots g * 128 to (g + 1) * 128 - 1. Of the 44 entries of the 4 block rows of one device (slots d * 4 to (d + 1) * 4 - 1), at most 2 name slots of any one device, and exactly 2 name slots of some device. `new_slot`: A permutation. On every device exactly one block row moves, from a slot k with 2 <= k % 4; it stays in its part, goes from owner b to owner b XOR m, where m (1 to 31) is one number for the whole part, and takes the slot that the moving row of that device leaves.
All inputs are finite; a program needn't handle non-finite values.
Results may differ from a plain program's by a relative error of at most 0.0003.
Values sent between devices are 32-bit elements; how exact they have to be, the bound alone decides.
A program may use at most 64 MiB of HBM per device.

v0:
```python
import jax
import jax.numpy as jnp
from jax import lax
from jax.sharding import PartitionSpec as P

highest = lax.Precision.HIGHEST
diagonal_shift = 4.0


def chol_apply(matrix, right):
    factor = jnp.linalg.cholesky(matrix)
    middle = lax.linalg.triangular_solve(factor, right, left_side=True, lower=True)
    return lax.linalg.triangular_solve(factor, middle, left_side=True, lower=True, transpose_a=True)


def gram(left, right):
    return jnp.einsum("snt,smt->nm", left, right, precision=highest)


def sym(m):
    return 0.5 * (m + m.T)


def mm(a, b):
    return jnp.dot(a, b, precision=highest)


def off_part(vectors, diag, masked, column_ids, coupling):
    boundary_rows = coupling.shape[0]
    part_count = coupling.shape[1]
    border = lax.all_gather(vectors[:boundary_rows], "group", axis=0, tiled=True)
    own = jnp.einsum("rnj,rij->rni", vectors, diag, precision=highest)
    returned = jnp.einsum("rni,rkij->rknj", vectors, masked, precision=highest)
    panel = lax.all_gather(vectors, "bulk", axis=0, tiled=True)
    picked = panel[column_ids]
    own = own + jnp.einsum("rknj,rkij->rni", picked, masked, precision=highest)
    border = border.reshape((part_count, boundary_rows) + vectors.shape[1:])
    crossed = jnp.einsum("khij,hknj->kni", coupling, border, precision=highest)
    return (own.at[:boundary_rows].add(crossed), returned.reshape((-1,) + vectors.shape[1:]), panel)


def coefficients(n0, n1, n2, n3):
    n = n0.shape[0]
    eye = jnp.eye(n, dtype=n0.dtype)
    n0, n1, n2, n3 = (sym(n0), sym(n1), sym(n2), sym(n3))
    delta = chol_apply(diagonal_shift * n0 + n1, n1)
    alpha = (eye - delta) / diagonal_shift
    b = -alpha
    cross = mm(delta.T, mm(n1, b))
    gram_new = sym(mm(delta.T, mm(n0, delta)) + cross + cross.T + mm(b.T, mm(n2, b)))
    beta = chol_apply(n0, gram_new)
    a = delta + beta
    c1 = mm(a.T, mm(n1, b))
    c2 = mm(a.T, mm(n2, b))
    pp = mm(a.T, mm(n0, a)) + c1 + c1.T + mm(b.T, mm(n2, b))
    pep = mm(a.T, mm(n1, a)) + c2 + c2.T + mm(b.T, mm(n3, b))
    alpha2 = chol_apply(sym(diagonal_shift * pp + pep), gram_new)
    ba = mm(b, alpha2)
    aa = mm(a, alpha2)
    sol = (alpha + aa, ba)
    res = (delta - diagonal_shift * aa, b - diagonal_shift * ba - aa, -ba)
    return (sol, res)


def local(rhs, diag_tiles, offdiag_blocks, coupling, col_index, load, new_slot):
    row_count = rhs.shape[0]
    off_count = offdiag_blocks.shape[1]
    bulk_count = lax.axis_size("bulk")
    group_rows = row_count * bulk_count
    group_base = lax.axis_index("group") * group_rows
    first = lax.axis_index("bulk") * row_count
    cols = lax.dynamic_slice_in_dim(col_index, group_base, group_rows) - group_base
    moved = lax.dynamic_slice_in_dim(new_slot, group_base, group_rows) - group_base
    loads = lax.dynamic_slice_in_dim(load, group_base + first, row_count)
    my_cols = lax.dynamic_slice_in_dim(cols, first, row_count)
    my_new = lax.dynamic_slice_in_dim(moved, first, row_count)
    tile_ids = jnp.arange(off_count, dtype=jnp.int32)
    mask = (tile_ids[None, :] < loads[:, None]).astype(jnp.float32)
    masked = offdiag_blocks * mask[:, :, None, None]
    u0 = rhs
    own, returned, panel0 = off_part(u0, diag_tiles, masked, my_cols, coupling)
    buffer = jax.ops.segment_sum(returned, my_cols.reshape(-1), num_segments=group_rows)
    u1 = own + lax.psum_scatter(buffer, "bulk", scatter_dimension=0, tiled=True)
    own, returned, panel1 = off_part(u1, diag_tiles, masked, my_cols, coupling)
    ids = jnp.concatenate([moved[my_cols.reshape(-1)], my_new])
    buffer = jax.ops.segment_sum(jnp.concatenate([returned, own]), ids, num_segments=group_rows)
    u2 = lax.psum_scatter(buffer, "bulk", scatter_dimension=0, tiled=True)
    inverse = jnp.zeros_like(moved).at[moved].set(jnp.arange(group_rows, dtype=jnp.int32))
    mine = lax.dynamic_slice_in_dim(inverse, first, row_count)
    v0, v1 = (panel0[mine], panel1[mine])
    grams = jnp.stack([gram(v0, v0), gram(v0, v1), gram(v1, v1), gram(v1, u2)])
    grams = lax.psum(grams, ("group", "bulk"))
    sol, res = coefficients(grams[0], grams[1], grams[2], grams[3])
    basis = jnp.concatenate([v0, v1, u2], axis=1)
    zero = jnp.zeros_like(sol[0])
    weights = jnp.concatenate(
        [jnp.concatenate(sol + (zero,), axis=0), jnp.concatenate(res, axis=0)], axis=1
    )
    out = jnp.einsum("mn,smt->snt", weights, basis, precision=highest)
    n = rhs.shape[1]
    return (out[:, :n], out[:, n:])


def solution(mesh):
    return jax.shard_map(
        local,
        mesh=mesh,
        in_specs=(
            P(("group", "bulk"), None, None),
            P(("group", "bulk"), None, None),
            P(("group", "bulk"), None, None, None),
            P(("group", "bulk"), None, None, None),
            P(),
            P(),
            P(),
        ),
        out_specs=(P(("group", "bulk"), None, None), P(("group", "bulk"), None, None)),
        check_vma=False,
    )
```

profile of v0, /device:TPU:1, one launch (start us, length us, event | category | flops | bytes accessed | tf_op | source)
XLA Modules:
  0.0 494.6 jit_solution(10182201475086260046)
XLA Ops:
  9.8 3.8 fusion.4
  16.0 6.9 %scatter_fusion = f32[128,64,128]{2,1,0:T(8,128)} fusion(f32[128,64,128]{2,1,0:T(8,128)} %broadcast.140.clone, s32[44]{0:T(128)S(1)} %reshape.206, f32[44,64,128]{2,1,0:T(8,128)S(1)} %bitcast.248), kind=kCustom, calls=%fused_computation.6 | custom fusion | flops 360448 | bytes 4325552 | tf_op jit(solution)/shard_map/scatter-add | solution.py:82
  25.9 12.7 %all_gather.13 = f32[8,64,128]{2,1,0:T(8,128)} all-gather(f32[2,64,128]{2,1,0:T(8,128)} %slice.81), channel_id=1, replica_groups=mesh['group'=4,'bulk'=32] {'group'}, dimensions={0}, use_global_device_ids=true | all-gather | bytes 327680 | tf_op jit(solution)/shard_map/all_gather | solution.py:31
  38.5 21.5 %all-gather.3.cloned.1.call-done = f32[128,64,128]{2,1,0:T(8,128)} async-done(((f32[4,64,128]{2,1,0:T(8,128)}), f32[128,64,128]{2,1,0:T(8,128)}) %all-gather.3.cloned.1.call-update) | async-done | bytes 4194320 | tf_op jit(solution)/shard_map/all_gather | solution.py:34
  60.1 4.0 gather_fusion.1
  64.1 4.8 fusion.12
  72.4 71.0 %reduce-scatter.3.cloned.1.call-done = f32[4,64,128]{2,1,0:T(8,128)} async-done(((f32[128,64,128]{2,1,0:T(8,128)}), f32[4,64,128]{2,1,0:T(8,128)}) %reduce-scatter.3.cloned.1.call-update) | async-done | bytes 131088 | tf_op jit(solution)/shard_map/reduce_scatter | solution.py:83
  147.7 10.6 %all_gather.15 = f32[8,64,128]{2,1,0:T(8,128)} all-gather(f32[2,64,128]{2,1,0:T(8,128)S(1)} %slice.102), channel_id=1, replica_groups=mesh['group'=4,'bulk'=32] {'group'}, dimensions={0}, use_global_device_ids=true | all-gather | bytes 327680 | tf_op jit(solution)/shard_map/all_gather | solution.py:31
  158.3 4.1 fusion.2
  162.4 31.4 %all-gather.5.cloned.1.call-done = f32[128,64,128]{2,1,0:T(8,128)} async-done(((f32[4,64,128]{2,1,0:T(8,128)}), f32[128,64,128]{2,1,0:T(8,128)}) %all-gather.5.cloned.1.call-update) | async-done | bytes 4194320 | tf_op jit(solution)/shard_map/all_gather | solution.py:34
  193.8 3.9 gather_fusion.4
  197.7 4.9 fusion.15
  204.1 2.5 broadcast.140
  206.6 6.9 %scatter_fusion.1 = f32[128,64,128]{2,1,0:T(8,128)} fusion(f32[128,64,128]{2,1,0:T(8,128)} %broadcast.140, s32[48]{0:T(128)S(1)} %pad_add_fusion, f32[48,64,128]{2,1,0:T(8,128)S(1)} %pad_maximum_fusion), kind=kCustom, calls=%fused_computation.7 | custom fusion | flops 393216 | bytes 4718784 | tf_op jit(solution)/shard_map/scatter-add | solution.py:86
  214.9 2.7 gather_fusion
  217.9 2.7 gather_fusion.2
  221.1 72.2 %reduce-scatter.5.cloned.1.call-done = f32[4,64,128]{2,1,0:T(8,128)} async-done(((f32[128,64,128]{2,1,0:T(8,128)}), f32[4,64,128]{2,1,0:T(8,128)}) %reduce-scatter.5.cloned.1.call-update) | async-done | bytes 131088 | tf_op jit(solution)/shard_map/reduce_scatter | solution.py:87
  295.2 146.3 %all-reduce.2.cloned.1.call-done = f32[4,64,64]{2,1,0:T(8,128)} async-done(((f32[4,64,64]{2,1,0:T(8,128)}), f32[4,64,64]{2,1,0:T(8,128)}) %all-reduce.2.cloned.1.call-update) | async-done | bytes 65552 | tf_op jit(solution)/shard_map/psum | solution.py:92
  443.6 5.9 %cholesky.59 = f32[64,64]{1,0:T(8,128)S(1)} custom-call(f32[64,64]{1,0:T(8,128)S(1)} %copy.82), custom_call_target="Cholesky" | custom-call | tf_op jit(solution)/shard_map/jit(cholesky)/cholesky | solution.py:11
  450.8 4.9 custom-call.13
  456.7 5.9 %cholesky.70 = f32[64,64]{1,0:T(8,128)S(1)} custom-call(f32[64,64]{1,0:T(8,128)S(1)} %copy.85), custom_call_target="Cholesky" | custom-call | tf_op jit(solution)/shard_map/jit(cholesky)/cholesky | solution.py:11
  463.9 4.9 custom-call.15
  473.9 5.8 %cholesky.81 = f32[64,64]{1,0:T(8,128)S(1)} custom-call(f32[64,64]{1,0:T(8,128)S(1)} %fusion.51), custom_call_target="Cholesky" | custom-call | tf_op jit(solution)/shard_map/jit(cholesky)/cholesky | solution.py:11
  481.1 4.9 custom-call.17
  (120 shorter events, 35.1 us)
Async XLA Ops:
  7.2 63.1 %copy-start = (f32[2,4,128,128]{3,2,1,0:T(8,128)S(1)}, f32[2,4,128,128]{3,2,1,0:T(8,128)}, u32[]{:S(2)}) copy-start(f32[2,4,128,128]{3,2,1,0:T(8,128)} %param.19) | copy-start | bytes 1572868
  7.2 52.9 %all-gather.3.cloned.1.call-start = ((), (), s32[]{:S(2)}) async-start(), calls=%async_computation.2 | async-start | bytes 4325376 | tf_op jit(solution)/shard_map/all_gather | solution.py:34
  7.9 135.5 %reduce-scatter.3.cloned.1.call-start = ((), (), s32[]{:S(2)}) async-start(), calls=%async_computation.3 | async-start | bytes 4325376 | tf_op jit(solution)/shard_map/reduce_scatter | solution.py:83
  22.9 0.9 copy-start.4
  22.9 41.2 %copy-start.1 = (f32[4,11,128,128]{3,2,1,0:T(8,128)S(1)}, f32[4,11,128,128]{3,2,1,0:T(8,128)}, u32[]{:S(2)}) copy-start(f32[4,11,128,128]{3,2,1,0:T(8,128)} %param.18) | copy-start | bytes 8650756
  22.9 170.9 %all-gather.5.cloned.1.call-start = ((), (), s32[]{:S(2)}) async-start(), calls=%async_computation.4 | async-start | bytes 4325376 | tf_op jit(solution)/shard_map/all_gather | solution.py:34
  64.1 4.8 copy-start.7
  64.1 6.1 %copy-start.6 = (f32[8,64,128]{2,1,0:T(8,128)S(1)}, f32[8,64,128]{2,1,0:T(8,128)}, u32[]{:S(2)}) copy-start(f32[8,64,128]{2,1,0:T(8,128)} %all_gather.13) | copy-start | bytes 786436
  145.0 148.3 %reduce-scatter.5.cloned.1.call-start = ((), (), s32[]{:S(2)}) async-start(), calls=%async_computation.5 | async-start | bytes 4325376 | tf_op jit(solution)/shard_map/reduce_scatter | solution.py:87
  197.7 4.9 copy-start.3
  197.7 4.9 %copy-start.8 = (f32[4,128,128]{2,1,0:T(8,128)S(1)}, f32[4,128,128]{2,1,0:T(8,128)}, u32[]{:S(2)}) copy-start(f32[4,128,128]{2,1,0:T(8,128)} %param.17) | copy-start | bytes 786436
  197.7 5.6 %copy-start.5 = (f32[8,64,128]{2,1,0:T(8,128)S(1)}, f32[8,64,128]{2,1,0:T(8,128)}, u32[]{:S(2)}) copy-start(f32[8,64,128]{2,1,0:T(8,128)} %all_gather.15) | copy-start | bytes 786436
  197.7 6.2 %copy-start.2 = (f32[4,11,128,64]{2,3,1,0:T(8,128)S(1)}, f32[4,11,128,64]{2,3,1,0:T(8,128)}, u32[]{:S(2)}) copy-start(f32[4,11,128,64]{2,3,1,0:T(8,128)} %fusion.2) | copy-start | bytes 4325380
  213.5 228.1 %all-reduce.2.cloned.1.call-start = ((), (), s32[]{:S(2)}) async-start(), calls=%async_computation.6 | async-start | bytes 262144 | tf_op jit(solution)/shard_map/psum | solution.py:92
  294.5 192.4 %copy-start.9 = (f32[4,64,128]{2,1,0:T(8,128)S(1)}, f32[4,64,128]{2,1,0:T(8,128)}, u32[]{:S(2)}) copy-start(f32[4,64,128]{2,1,0:T(8,128)} %reduce-scatter.5.cloned.1.call-done) | copy-start | bytes 393220
Sparse Core Ops, SparseCore 0:
  10.2 49.7 all-gather.2
  63.7 79.6 reduce-scatter.2
  146.2 47.5 all-gather.4
  213.6 79.7 reduce-scatter.4
  298.5 142.9 all-reduce.1
where the time goes:
time: 496 us; the launch traced here: 495 us
  waiting for transfers between devices  343 us (69%)
  other arithmetic  55.1 us (11%)
  matrix products  30.5 us (6%)
  local copies, waits for them, and re-layouts  28.1 us (6%)
  blocking collectives  23.2 us (5%)
  between operations  14.3 us (3%)
    psum x1, waiting for transfers between devices, local(): grams = lax.psum(grams, ('group', 'bulk'))  146 us
    reduce_scatter x1, waiting for transfers between devices, local(): u2 = lax.psum_scatter(buffer, 'bulk', scatter_dimension=0, tiled=True)  72.2 us
    reduce_scatter x1, waiting for transfers between devices, local(): u1 = own + lax.psum_scatter(buffer, 'bulk', scatter_dimension=0, tiled=True)  71 us
    all_gather x2, waiting for transfers between devices, off_part(): panel = lax.all_gather(vectors, 'bulk', axis=0, tiled=True)  52.9 us
    all_gather x2, blocking collectives, off_part(): lax.all_gather(vectors[:boundary_rows], 'group', axis=0, tiled=True)  23.2 us
    another operation x9, other arithmetic, chol_apply(): factor = jnp.linalg.cholesky(matrix)  19.6 us
    another operation x6, other arithmetic, chol_apply(): lax.linalg.triangular_solve(factor, middle, left_side=True, lower=True, t...  16.6 us
  transfers between devices with their start and end apart: 5, of which 5 were waited for; matrix products, arithmetic and copies ran while one was open for 9% of the time, Pallas kernels for 0%

commit v1 on v0

--- a/solution.py
+++ b/solution.py
@@ -89,7 +89,7 @@
     mine = lax.dynamic_slice_in_dim(inverse, first, row_count)
     v0, v1 = (panel0[mine], panel1[mine])
     grams = jnp.stack([gram(v0, v0), gram(v0, v1), gram(v1, v1), gram(v1, u2)])
-    grams = lax.psum(grams, ("group", "bulk"))
+    grams = jnp.sum(lax.all_gather(grams, ("group", "bulk")), axis=0)
     sol, res = coefficients(grams[0], grams[1], grams[2], grams[3])
     basis = jnp.concatenate([v0, v1, u2], axis=1)
     zero = jnp.zeros_like(sol[0])

time: 496 us -> 437 us (0.88)
  waiting for transfers between devices: 343 us -> 280 us
  other arithmetic: 55.1 us -> 61.8 us
    psum x1 -> x0, waiting for transfers between devices: 146 us -> none  [local(): grams = lax.psum(grams, ('group', 'bulk'))]
    all_gather x0 -> x1, waiting for transfers between devices: none -> 83 us  [local(): grams = jnp.sum(lax.all_gather(grams, ('group', 'bulk')), axis=0)]
    reduce_sum x0 -> x1, other arithmetic: none -> 7.53 us  [local(): grams = jnp.sum(lax.all_gather(grams, ('group', 'bulk')), axis=0)]
  transfers between devices with their start and end apart: 5 -> 5, of which waited for: 5 -> 5; matrix products, arithmetic and copies ran while one was open for 9% -> 10% of each run, Pallas kernels for 0% -> 0%
where the time goes in v1:
time: 437 us; the launch traced here: 436 us
  waiting for transfers between devices  280 us (64%)
  other arithmetic  61.8 us (14%)
  matrix products  29 us (7%)
  local copies, waits for them, and re-layouts  27.3 us (6%)
  blocking collectives  23.2 us (5%)
  between operations  14.3 us (3%)
    all_gather x1, waiting for transfers between devices, local(): grams = jnp.sum(lax.all_gather(grams, ('group', 'bulk')), axis=0)  83 us
    reduce_scatter x1, waiting for transfers between devices, local(): u2 = lax.psum_scatter(buffer, 'bulk', scatter_dimension=0, tiled=True)  72.2 us
    reduce_scatter x1, waiting for transfers between devices, local(): u1 = own + lax.psum_scatter(buffer, 'bulk', scatter_dimension=0, tiled=True)  71 us
    all_gather x2, waiting for transfers between devices, off_part(): panel = lax.all_gather(vectors, 'bulk', axis=0, tiled=True)  52.9 us
    all_gather x2, blocking collectives, off_part(): lax.all_gather(vectors[:boundary_rows], 'group', axis=0, tiled=True)  23.2 us
    another operation x9, other arithmetic, chol_apply(): factor = jnp.linalg.cholesky(matrix)  19.6 us
    another operation x6, other arithmetic, chol_apply(): lax.linalg.triangular_solve(factor, middle, left_side=True, lower=True, t...  16.6 us
    dot_general x2, matrix products, off_part(): own = own + jnp.einsum('rknj,rkij->rni', picked, masked, precision=highest)  9.75 us
  transfers between devices with their start and end apart: 5, of which 5 were waited for; matrix products, arithmetic and copies ran while one was open for 10% of the time, Pallas kernels for 0%

profile of v1, /device:TPU:1, one launch (start us, length us, event | category | flops | bytes accessed | tf_op | source)
XLA Modules:
  0.0 435.8 jit_solution(12975206923112830053)
XLA Ops:
  9.8 3.8 fusion.4
  16.0 6.9 %scatter_fusion = f32[128,64,128]{2,1,0:T(8,128)} fusion(f32[128,64,128]{2,1,0:T(8,128)} %broadcast.140.clone, s32[44]{0:T(128)S(1)} %reshape.206, f32[44,64,128]{2,1,0:T(8,128)S(1)} %bitcast.250), kind=kCustom, calls=%fused_computation.6 | custom fusion | flops 360448 | bytes 4325552 | tf_op jit(solution)/shard_map/scatter-add | solution.py:82
  25.9 12.7 %all_gather.19 = f32[8,64,128]{2,1,0:T(8,128)} all-gather(f32[2,64,128]{2,1,0:T(8,128)} %slice.81), channel_id=1, replica_groups=mesh['group'=4,'bulk'=32] {'group'}, dimensions={0}, use_global_device_ids=true | all-gather | bytes 327680 | tf_op jit(solution)/shard_map/all_gather | solution.py:31
  38.5 21.5 %all-gather.5.cloned.1.call-done = f32[128,64,128]{2,1,0:T(8,128)} async-done(((f32[4,64,128]{2,1,0:T(8,128)}), f32[128,64,128]{2,1,0:T(8,128)}) %all-gather.5.cloned.1.call-update) | async-done | bytes 4194320 | tf_op jit(solution)/shard_map/all_gather | solution.py:34
  60.1 4.0 gather_fusion.1
  64.1 4.8 %fusion.12 = f32[4,64,128]{2,1,0:T(8,128)S(1)} fusion(f32[4,11,64,128]{3,2,1,0:T(8,128)} %bitcast.252, f32[4,11,128,128]{3,2,1,0:T(8,128)S(1)} %copy-done.1, f32[4,11]{1,0:T(4,128)S(1)} %fusion.85), kind=kOutput, calls=%fused_computation.22 | convolution fusion | flops 554369024 | bytes 4456624 | tf_op jit(solution)/shard_map/rknj,rkij->rni/dot_general | solution.py:36
  72.4 71.0 %reduce-scatter.3.cloned.1.call-done = f32[4,64,128]{2,1,0:T(8,128)} async-done(((f32[128,64,128]{2,1,0:T(8,128)}), f32[4,64,128]{2,1,0:T(8,128)}) %reduce-scatter.3.cloned.1.call-update) | async-done | bytes 131088 | tf_op jit(solution)/shard_map/reduce_scatter | solution.py:83
  147.7 10.6 %all_gather.21 = f32[8,64,128]{2,1,0:T(8,128)} all-gather(f32[2,64,128]{2,1,0:T(8,128)S(1)} %slice.102), channel_id=1, replica_groups=mesh['group'=4,'bulk'=32] {'group'}, dimensions={0}, use_global_device_ids=true | all-gather | bytes 327680 | tf_op jit(solution)/shard_map/all_gather | solution.py:31
  158.3 4.1 fusion.2
  162.4 31.4 %all-gather.7.cloned.1.call-done = f32[128,64,128]{2,1,0:T(8,128)} async-done(((f32[4,64,128]{2,1,0:T(8,128)}), f32[128,64,128]{2,1,0:T(8,128)}) %all-gather.7.cloned.1.call-update) | async-done | bytes 4194320 | tf_op jit(solution)/shard_map/all_gather | solution.py:34
  193.8 3.9 gather_fusion.4
  197.7 4.9 %fusion.15 = f32[4,64,128]{2,1,0:T(8,128)S(1)} fusion(f32[4,11,64,128]{3,2,1,0:T(8,128)} %bitcast.251, f32[4,11,128,128]{3,2,1,0:T(8,128)S(1)} %copy-done.1, f32[4,11]{1,0:T(4,128)S(1)} %fusion.85), kind=kOutput, calls=%fused_computation.23 | convolution fusion | flops 554369024 | bytes 4456624 | tf_op jit(solution)/shard_map/rknj,rkij->rni/dot_general | solution.py:36
  206.6 6.9 %scatter_fusion.1 = f32[128,64,128]{2,1,0:T(8,128)} fusion(f32[128,64,128]{2,1,0:T(8,128)} %broadcast.140, s32[48]{0:T(128)S(1)} %pad_add_fusion, f32[48,64,128]{2,1,0:T(8,128)S(1)} %pad_maximum_fusion), kind=kCustom, calls=%fused_computation.7 | custom fusion | flops 393216 | bytes 4718784 | tf_op jit(solution)/shard_map/scatter-add | solution.py:86
  214.9 2.7 gather_fusion
  217.9 2.7 gather_fusion.2
  221.1 72.2 %reduce-scatter.5.cloned.1.call-done = f32[4,64,128]{2,1,0:T(8,128)} async-done(((f32[128,64,128]{2,1,0:T(8,128)}), f32[4,64,128]{2,1,0:T(8,128)}) %reduce-scatter.5.cloned.1.call-update) | async-done | bytes 131088 | tf_op jit(solution)/shard_map/reduce_scatter | solution.py:87
  295.2 83.0 %all-gather.9.cloned.1.call-done = f32[512,64,64]{2,1,0:T(8,128)} async-done(((f32[4,64,64]{2,1,0:T(8,128)}), f32[512,64,64]{2,1,0:T(8,128)}) %all-gather.9.cloned.1.call-update) | async-done | bytes 8388624 | tf_op jit(solution)/shard_map/all_gather | solution.py:92
  378.3 7.5 %reduce_sum.9 = f32[4,64,64]{2,1,0:T(8,128)S(1)} reduce(f32[128,4,64,64]{3,2,1,0:T(8,128)} %bitcast.248, f32[]{:T(128)} %constant.110.clone.1), dimensions={0}, to_apply=%region_5.0 | reduce | flops 2080768 | bytes 8454148 | tf_op jit(solution)/shard_map/reduce_sum | solution.py:92
  386.3 5.9 %cholesky.59 = f32[64,64]{1,0:T(8,128)S(1)} custom-call(f32[64,64]{1,0:T(8,128)S(1)} %copy.82), custom_call_target="Cholesky" | custom-call | tf_op jit(solution)/shard_map/jit(cholesky)/cholesky | solution.py:11
  393.5 4.9 %custom-call.13 = f32[1,64,64]{1,2,0:T(8,128)S(1)} custom-call(f32[1,64,64]{2,1,0:T(8,128)S(1)} %fusion.41), custom_call_target="InvertDiagBlocksLowerTriangular" | custom-call | tf_op jit(solution)/shard_map/triangular_solve/custom-call.2 | solution.py:13
  399.4 5.9 %cholesky.70 = f32[64,64]{1,0:T(8,128)S(1)} custom-call(f32[64,64]{1,0:T(8,128)S(1)} %copy.85), custom_call_target="Cholesky" | custom-call | tf_op jit(solution)/shard_map/jit(cholesky)/cholesky | solution.py:11
  406.6 4.9 %custom-call.15 = f32[1,64,64]{1,2,0:T(8,128)S(1)} custom-call(f32[1,64,64]{2,1,0:T(8,128)S(1)} %fusion.42), custom_call_target="InvertDiagBlocksLowerTriangular" | custom-call | tf_op jit(solution)/shard_map/triangular_solve/custom-call.2 | solution.py:13
  415.1 5.8 %cholesky.81 = f32[64,64]{1,0:T(8,128)S(1)} custom-call(f32[64,64]{1,0:T(8,128)S(1)} %fusion.51), custom_call_target="Cholesky" | custom-call | tf_op jit(solution)/shard_map/jit(cholesky)/cholesky | solution.py:11
  422.3 4.9 %custom-call.17 = f32[1,64,64]{1,2,0:T(8,128)S(1)} custom-call(f32[1,64,64]{2,1,0:T(8,128)S(1)} %fusion.43), custom_call_target="InvertDiagBlocksLowerTriangular" | custom-call | tf_op jit(solution)/shard_map/triangular_solve/custom-call.2 | solution.py:13
  (121 shorter events, 34.5 us)
Async XLA Ops:
  7.2 63.1 %copy-start = (f32[2,4,128,128]{3,2,1,0:T(8,128)S(1)}, f32[2,4,128,128]{3,2,1,0:T(8,128)}, u32[]{:S(2)}) copy-start(f32[2,4,128,128]{3,2,1,0:T(8,128)} %param.19) | copy-start | bytes 1572868
  7.2 52.9 %all-gather.5.cloned.1.call-start = ((), (), s32[]{:S(2)}) async-start(), calls=%async_computation.2 | async-start | bytes 4325376 | tf_op jit(solution)/shard_map/all_gather | solution.py:34
  7.9 135.5 %reduce-scatter.3.cloned.1.call-start = ((), (), s32[]{:S(2)}) async-start(), calls=%async_computation.3 | async-start | bytes 4325376 | tf_op jit(solution)/shard_map/reduce_scatter | solution.py:83
  22.9 0.9 copy-start.4
  22.9 41.2 %copy-start.1 = (f32[4,11,128,128]{3,2,1,0:T(8,128)S(1)}, f32[4,11,128,128]{3,2,1,0:T(8,128)}, u32[]{:S(2)}) copy-start(f32[4,11,128,128]{3,2,1,0:T(8,128)} %param.18) | copy-start | bytes 8650756
  22.9 170.9 %all-gather.7.cloned.1.call-start = ((), (), s32[]{:S(2)}) async-start(), calls=%async_computation.4 | async-start | bytes 4325376 | tf_op jit(solution)/shard_map/all_gather | solution.py:34
  64.1 4.8 %copy-start.7 = (f32[4,128,128]{2,1,0:T(8,128)S(1)}, f32[4,128,128]{2,1,0:T(8,128)}, u32[]{:S(2)}) copy-start(f32[4,128,128]{2,1,0:T(8,128)} %param.17) | copy-start | bytes 786436
  64.1 6.1 %copy-start.6 = (f32[8,64,128]{2,1,0:T(8,128)S(1)}, f32[8,64,128]{2,1,0:T(8,128)}, u32[]{:S(2)}) copy-start(f32[8,64,128]{2,1,0:T(8,128)} %all_gather.19) | copy-start | bytes 786436
  145.0 148.3 %reduce-scatter.5.cloned.1.call-start = ((), (), s32[]{:S(2)}) async-start(), calls=%async_computation.5 | async-start | bytes 4325376 | tf_op jit(solution)/shard_map/reduce_scatter | solution.py:87
  197.7 4.9 %copy-start.3 = (f32[4,64,128]{2,1,0:T(8,128)S(1)}, f32[4,64,128]{2,1,0:T(8,128)}, u32[]{:S(2)}) copy-start(f32[4,64,128]{2,1,0:T(8,128)} %add.179) | copy-start | bytes 393220
  197.7 4.9 %copy-start.8 = (f32[4,128,128]{2,1,0:T(8,128)S(1)}, f32[4,128,128]{2,1,0:T(8,128)}, u32[]{:S(2)}) copy-start(f32[4,128,128]{2,1,0:T(8,128)} %param.17) | copy-start | bytes 786436
  197.7 5.6 %copy-start.5 = (f32[8,64,128]{2,1,0:T(8,128)S(1)}, f32[8,64,128]{2,1,0:T(8,128)}, u32[]{:S(2)}) copy-start(f32[8,64,128]{2,1,0:T(8,128)} %all_gather.21) | copy-start | bytes 786436
  197.7 6.2 %copy-start.2 = (f32[4,11,128,64]{2,3,1,0:T(8,128)S(1)}, f32[4,11,128,64]{2,3,1,0:T(8,128)}, u32[]{:S(2)}) copy-start(f32[4,11,128,64]{2,3,1,0:T(8,128)} %fusion.2) | copy-start | bytes 4325380
  213.5 164.8 %all-gather.9.cloned.1.call-start = ((), (), s32[]{:S(2)}) async-start(), calls=%async_computation.6 | async-start | bytes 16908288 | tf_op jit(solution)/shard_map/all_gather | solution.py:92
  385.8 42.3 %copy-start.9 = (f32[4,64,128]{2,1,0:T(8,128)S(1)}, f32[4,64,128]{2,1,0:T(8,128)}, u32[]{:S(2)}) copy-start(f32[4,64,128]{2,1,0:T(8,128)} %reduce-scatter.5.cloned.1.call-done) | copy-start | bytes 393220
Sparse Core Ops, SparseCore 0:
  10.2 49.7 all-gather.4
  63.7 79.6 reduce-scatter.2
  146.2 47.5 all-gather.6
  213.6 79.7 reduce-scatter.4
  296.9 81.2 all-gather.8
